TPU v7x, 128 devices: a whole 4x4x4 slice. The times are simulated.
128 devices in a mesh: mode: 32 (over x, y, core), wall: 2 (over z_lo), ckpt: 2 (over z_hi).
Axes of the slice: x: 4, y: 4, z: 4 (z_hi: 2, z_lo: 2; z = z_hi * 2 + z_lo), core: 2. Of those that a mesh axis runs over, the one named last changes fastest.
Arguments:
- adjoint: float32 [2, 5, 1024, 4096], P(None, None, ('wall', 'ckpt'), 'mode'), may hold values from -6 to 6
- forward: float32 [2, 2, 1024, 4096], P('ckpt', None, 'wall', 'mode'), may hold values from -0.09375 to 0.09375
- mode_map: int32 [4096], P('mode'), may hold values from 0 to 4095, as said below
Outputs:
- adjoint_prev: float32 [2, 5, 1024, 4096], P(None, None, ('wall', 'ckpt'), 'mode')
Inputs may be any that keep to these rules, and one draw needn't show every extreme that they name: mode_map is a permutation of the 64 x 64 modes laid out by frequency: for every block b of 64 consecutive slots there is a frequency p(b) such that slot b * 64 + r holds mode p(b) * 64 + r, and p takes every frequency once.
All inputs are finite; a program needn't handle non-finite values.
Results may differ from a plain program's by a relative error of at most 0.0001.
Values sent between devices are 32-bit elements; how exact they have to be, the bound alone decides.
A program may use at most 128 MiB of HBM per device.

v0:
```python
import math
import jax
import jax.numpy as jnp
from jax import lax
from jax.sharding import PartitionSpec as P

NF = 64
NK = 64
MODES = 4096
KAPPA = 0.2
COUPLING = 0.5
HIGHEST = lax.Precision.HIGHEST


def with_halo(block, sides, width):
    for axis, dim in sides:
        count = lax.axis_size(axis)
        forward = [(i, i + 1) for i in range(count - 1)]
        backward = [(target, source) for source, target in forward]
        low = lax.ppermute(
            lax.slice_in_dim(block, block.shape[dim] - width, None, axis=dim), axis, forward
        )
        high = lax.ppermute(lax.slice_in_dim(block, 0, width, axis=dim), axis, backward)
        block = jnp.concatenate([low, block, high], axis=dim)
    return block


def entering(value, axis, join, neutral):
    count, mine = (lax.axis_size(axis), lax.axis_index(axis))
    pieces = lax.all_gather(value, axis)
    so_far = jnp.full_like(value, 0) + jnp.asarray(neutral, value.dtype)

    def turn(position, so_far):
        longer = join(so_far, pieces[position])
        return jnp.where(position < mine, longer, so_far)

    return lax.fori_loop(0, count - 1, turn, so_far)


def add_pair(earlier, later):
    return earlier + later


def rates(grid_index):
    freq_index = grid_index // NK
    span_index = grid_index % NK
    freq_signed = (freq_index + NF // 2) % NF - NF // 2
    span_signed = (span_index + NK // 2) % NK - NK // 2
    return (2.0 / NF * freq_signed.astype(jnp.float32), 2.0 / NK * span_signed.astype(jnp.float32))


def span_tables(direction):
    col_ids = jnp.arange(NK, dtype=jnp.int32)
    phase_cols = 2.0 * math.pi / NK * (col_ids[:, None] * col_ids[None, :] % NK).astype(jnp.float32)
    return (jnp.cos(phase_cols), direction * jnp.sin(phase_cols))


def row_tables(direction, out_ids, in_ids):
    phase_rows = 2.0 * math.pi / NF * (out_ids[:, None] * in_ids[None, :] % NF).astype(jnp.float32)
    return (jnp.cos(phase_rows), direction * jnp.sin(phase_rows))


def span_dft(real_part, imag_part, direction):
    cosine, sine_part = span_tables(direction)
    real_cos = jnp.einsum("...k,kz->...z", real_part, cosine, precision=HIGHEST)
    real_sin = jnp.einsum("...k,kz->...z", real_part, sine_part, precision=HIGHEST)
    imag_cos = jnp.einsum("...k,kz->...z", imag_part, cosine, precision=HIGHEST)
    imag_sin = jnp.einsum("...k,kz->...z", imag_part, sine_part, precision=HIGHEST)
    return (real_cos - imag_sin, real_sin + imag_cos)


def lead_dft(real_part, imag_part, direction, out_ids, in_ids):
    cos_rows, sin_rows = row_tables(direction, out_ids, in_ids)
    lead_shape = real_part.shape
    flat_real = real_part.reshape(lead_shape[0], -1)
    flat_imag = imag_part.reshape(lead_shape[0], -1)
    out_real = jnp.dot(cos_rows, flat_real, precision=HIGHEST) - jnp.dot(
        sin_rows, flat_imag, precision=HIGHEST
    )
    out_imag = jnp.dot(sin_rows, flat_real, precision=HIGHEST) + jnp.dot(
        cos_rows, flat_imag, precision=HIGHEST
    )
    return (out_real.reshape(lead_shape), out_imag.reshape(lead_shape))


def to_physical(real_part, imag_part, out_ids, in_ids):
    shape_front = real_part.shape[:-1] + (NF, NK)
    span_real, span_imag = span_dft(
        real_part.reshape(shape_front), imag_part.reshape(shape_front), 1.0
    )
    span_real = jnp.moveaxis(span_real, -2, 0)
    span_imag = jnp.moveaxis(span_imag, -2, 0)
    return lead_dft(span_real, span_imag, 1.0, out_ids, in_ids)


def to_spectral(real_part, imag_part, out_ids, in_ids):
    lead_real, lead_imag = lead_dft(real_part, imag_part, -1.0, out_ids, in_ids)
    lead_real = jnp.moveaxis(lead_real, 0, -2)
    lead_imag = jnp.moveaxis(lead_imag, 0, -2)
    span_real, span_imag = span_dft(lead_real, lead_imag, -1.0)
    shape_front = span_real.shape[:-2] + (MODES,)
    return (span_real.reshape(shape_front), span_imag.reshape(shape_front))


def coupling_term(adjoint_slots, forward_phys, block_freq, time_ids):
    a_real, a_imag = to_physical(adjoint_slots[0], adjoint_slots[1], time_ids, block_freq)
    w_real = forward_phys[0][:, None]
    w_imag = forward_phys[1][:, None]
    prod_real = w_real * a_real + w_imag * a_imag
    prod_imag = w_real * a_imag - w_imag * a_real
    real_part, imag_part = to_spectral(prod_real, prod_imag, block_freq, time_ids)
    return jnp.stack([real_part, imag_part]) / (NF * NK)


def add_continuity(stepped, running, row_scale):
    updated_v = jnp.stack(
        [stepped[0, 1] + running[1] * row_scale, stepped[1, 1] - running[0] * row_scale]
    )
    return jnp.concatenate([stepped[:, :1], updated_v[:, None], stepped[:, 2:]], 1)


def wall_step_modes(current, coupled, alpha_rate, beta_rate, row_scale):
    padded = with_halo(current, ((("wall", "ckpt"), 2),), 1)
    stepped = (
        current
        + KAPPA * (padded[:, :, 2:] - 2.0 * current + padded[:, :, :-2])
        - COUPLING * coupled
    )
    source = alpha_rate * stepped[:, 0] + beta_rate * stepped[:, 2]
    row_count = current.shape[2]
    row_ids = jnp.arange(row_count, dtype=jnp.int32)
    lower_ones = (row_ids[:, None] >= row_ids[None, :]).astype(jnp.float32)
    running = jnp.einsum("yv,cvm->cym", lower_ones, source, precision=HIGHEST)
    totals = running[:, -1]
    before = entering(totals, ("wall", "ckpt"), add_pair, jnp.zeros_like(totals))
    running = running + before[:, None]
    return add_continuity(stepped, running, row_scale)


def to_modes(values):
    return lax.all_to_all(values, "mode", split_axis=3, concat_axis=2, tiled=True)


def on_device(adjoint, forward, mode_map):
    station_count = lax.axis_size("ckpt")
    row_scale = 1.0 / math.sqrt(adjoint.shape[2] * lax.axis_size("wall") * lax.axis_size("ckpt"))
    stored = lax.all_gather(forward, "ckpt", axis=0, tiled=True)
    row_count = adjoint.shape[2]
    own_rows = lax.dynamic_slice_in_dim(stored, lax.axis_index("ckpt") * row_count, row_count, 2)
    full_map = lax.all_gather(mode_map, "mode", axis=0, tiled=True)
    block_freq = full_map.reshape(NF, NK)[:, 0] // NK
    time_ids = jnp.arange(NF, dtype=jnp.int32)
    adjoint_cols, forward_cols = (
        lax.all_to_all(adjoint, "mode", split_axis=2, concat_axis=3, tiled=True),
        lax.all_to_all(own_rows, "mode", split_axis=2, concat_axis=3, tiled=True),
    )
    phys_real, phys_imag = to_physical(forward_cols[:, 0], forward_cols[:, 1], time_ids, block_freq)
    local_alpha, local_beta = rates(mode_map)
    current = adjoint
    for station in range(station_count - 1, -1, -1):
        if station == station_count - 1:
            columns = adjoint_cols
        else:
            columns = lax.all_to_all(current, "mode", split_axis=2, concat_axis=3, tiled=True)
        station_phys = (phys_real[:, station], phys_imag[:, station])
        coupled = to_modes(coupling_term(columns, station_phys, block_freq, time_ids))
        current = wall_step_modes(current, coupled, local_alpha, local_beta, row_scale)
    return current


def solution(mesh):
    placed = (P(None, None, ("wall", "ckpt"), "mode"), P("ckpt", None, "wall", "mode"), P("mode"))
    return jax.shard_map(
        on_device,
        mesh=mesh,
        in_specs=placed,
        out_specs=P(None, None, ("wall", "ckpt"), "mode"),
        check_vma=False,
    )
```

profile of v0, /device:TPU:0, one launch (start us, length us, event | category | flops | bytes accessed | tf_op | source)
XLA Modules:
  0.0 545.5 jit_solution(10773207464401871965)
XLA Ops:
  6.5 3.5 copy.215
  10.0 7.6 %all-to-all-start.1 = ((f32[2,5,256,128]{3,1,0,2:T(8,128)}), f32[2,5,256,128]{3,1,0,2:T(8,128)S(1)}, u32[]{:S(2)}, u32[]{:S(2)}) async-start(f32[2,5,256,128]{3,1,0,2:T(8,128)} %copy.215), calls=%async_computation.1 | async-start | bytes 4194304 | tf_op jit(solution)/shard_map/all_to_all | solution.py:154
  18.3 40.0 %all-gather.2 = s32[32,1,128]{2,1,0:T(1,128)S(1)} all-gather(s32[1,1,128]{2,1,0:T(1,128)S(1)} %bitcast.305), channel_id=1, replica_groups=mesh['mode'=32,'wall'=2,'ckpt'=2] {'mode'}, dimensions={0}, use_global_device_ids=true | all-gather | bytes 16896 | tf_op jit(solution)/shard_map/all_gather | solution.py:150
  62.0 5.8 %all-to-all-start = ((f32[2,2,256,128]{3,1,0,2:T(2,128)}), f32[2,2,256,128]{3,1,0,2:T(2,128)}, u32[]{:S(2)}, u32[]{:S(2)}) async-start(f32[2,2,256,128]{3,1,0,2:T(2,128)} %copy.211), calls=%async_computation | async-start | bytes 1048576 | tf_op jit(solution)/shard_map/all_to_all | solution.py:155
  68.9 5.1 fusion.64
  74.0 5.1 fusion.76
  80.5 4.0 convolution_subtract_fusion.7
  84.5 4.0 convolution_add_fusion.7
  92.4 2.5 convolution_add_fusion.3
  113.1 3.2 multiply_subtract_fusion.1
  120.4 2.4 fusion.21
  127.3 3.7 convolution_subtract_fusion.6
  132.7 2.4 convolution_add_fusion.6
  137.0 17.9 %copy.223 = f32[2,5,8,4096]{2,0,1,3:T(2,128)} copy(f32[2,5,8,4096]{3,2,1,0:T(8,128)S(1)} %maximum_multiply_fusion) | data formatting | bytes 2621440 | tf_op jit(solution)/shard_map/div | solution.py:112
  154.8 31.2 %reshape.142 = f32[32,1,10240]{2,1,0:T(1,128)} reshape(f32[4096,5,2,8]{3,2,1,0:T(2,128)} %bitcast.284) | data formatting | bytes 2621440
  186.0 7.6 %all-to-all-start.2 = ((f32[32,1,10240]{2,1,0:T(1,128)}), f32[32,1,10240]{2,1,0:T(1,128)}, u32[]{:S(2)}, u32[]{:S(2)}) async-start(f32[32,1,10240]{2,1,0:T(1,128)} %reshape.142), calls=%async_computation.2 | async-start | bytes 2621440 | tf_op jit(solution)/shard_map/all_to_all | solution.py:141
  194.9 6.4 %collective-permute-start.1 = (f32[2,5,1,128]{3,0,2,1:T(2,128)S(1)}, f32[2,5,1,128]{3,0,2,1:T(2,128)S(1)}, u32[]{:S(2)}, u32[]{:S(2)}) collective-permute-start(f32[2,5,1,128]{3,0,2,1:T(2,128)S(1)} %copy.261), channel_id=1, source_target_pairs={{0,1},{1,2},{2,3},{4,5},{5,6},{6,7},{8,9},{9,10},{10,11},{12,13},{... | collective-permute-start | bytes 15368 | tf_op jit(solution)/shard_map/ppermute | solution.py:20
  203.8 9.6 %all-to-all-done.2 = f32[32,1,10240]{2,1,0:T(1,128)} async-done(((f32[32,1,10240]{2,1,0:T(1,128)}), f32[32,1,10240]{2,1,0:T(1,128)}, u32[]{:S(2)}, u32[]{:S(2)}) %all-to-all-start.2) | async-done | bytes 1310752 | tf_op jit(solution)/shard_map/all_to_all | solution.py:141
  213.9 5.1 reduce.4
  219.0 41.4 %reshape.143 = f32[4096,5,2,8]{3,2,1,0:T(2,128)} reshape(f32[32,10240]{1,0:T(8,128)S(1)} %reduce.4) | data formatting | bytes 2621440
  260.4 21.6 %copy.224 = f32[2,5,8,4096]{3,2,1,0:T(8,128)S(1)} copy(f32[2,5,8,4096]{2,0,1,3:T(2,128)} %bitcast.285) | data formatting | bytes 2621440 | tf_op jit(solution)/shard_map/all_to_all | solution.py:141
  284.6 2.4 fusion.9
  287.6 11.3 %all-gather = f32[8,1,128]{2,1,0:T(1,128)S(1)} all-gather(f32[2,1,128]{2,1,0:T(1,128)S(1)} %copy.227), channel_id=2, replica_groups=mesh['mode'=32,'wall'=2,'ckpt'=2] {'wall','ckpt'}, dimensions={0}, use_global_device_ids=true | all-gather | bytes 5120 | tf_op jit(solution)/shard_map/all_gather | solution.py:30
  302.0 4.1 all-to-all-start.3
  308.3 2.5 mul.490
  312.8 2.5 mul.494
  315.3 10.4 %all-to-all-done.3 = f32[2,5,256,128]{3,0,1,2:T(2,128)S(1)} async-done(((f32[2,5,256,128]{3,0,1,2:T(2,128)}), f32[2,5,256,128]{3,0,1,2:T(2,128)S(1)}, u32[]{:S(2)}, u32[]{:S(2)}) %all-to-all-start.3) | async-done | bytes 1310752 | tf_op jit(solution)/shard_map/all_to_all | solution.py:164
  329.1 2.4 fusion.79
  331.5 2.4 fusion.69
  336.1 2.6 fusion
  340.6 2.5 reshape.116
  343.0 2.9 fusion.141
  362.6 2.4 fusion.15
  365.0 2.4 fusion.13
  370.5 3.7 convolution_subtract_fusion.4
  374.3 2.6 stack_reshape.14
  376.9 3.7 convolution_add_fusion.4
  380.6 2.6 stack_reshape.15
  384.5 17.9 %copy.240 = f32[2,5,8,4096]{2,0,1,3:T(2,128)} copy(f32[2,5,8,4096]{3,2,1,0:T(8,128)S(1)} %maximum_multiply_fusion.1) | data formatting | bytes 2621440 | tf_op jit(solution)/shard_map/div | solution.py:112
  402.4 31.4 %reshape.144 = f32[32,1,10240]{2,1,0:T(1,128)} reshape(f32[4096,5,2,8]{3,2,1,0:T(2,128)} %bitcast.286) | data formatting | bytes 2621440
  433.8 4.0 all-to-all-start.4
  442.9 6.1 %collective-permute-start.3 = (f32[2,5,1,128]{3,0,2,1:T(2,128)S(1)}, f32[2,5,1,128]{3,0,2,1:T(2,128)S(1)}, u32[]{:S(2)}, u32[]{:S(2)}) collective-permute-start(f32[2,5,1,128]{3,0,2,1:T(2,128)S(1)} %copy.230), channel_id=1, source_target_pairs={{0,1},{1,2},{2,3},{4,5},{5,6},{6,7},{8,9},{9,10},{10,11},{12,13},{... | collective-permute-start | bytes 15368 | tf_op jit(solution)/shard_map/ppermute | solution.py:20
  451.4 6.1 %all-to-all-done.4 = f32[32,1,10240]{2,1,0:T(1,128)S(1)} async-done(((f32[32,1,10240]{2,1,0:T(1,128)}), f32[32,1,10240]{2,1,0:T(1,128)S(1)}, u32[]{:S(2)}, u32[]{:S(2)}) %all-to-all-start.4) | async-done | bytes 1310752 | tf_op jit(solution)/shard_map/all_to_all | solution.py:141
  457.5 3.7 reduce.5
  461.2 41.1 %reshape.145 = f32[4096,5,2,8]{3,2,1,0:T(2,128)} reshape(f32[32,10240]{1,0:T(8,128)S(1)} %reduce.5) | data formatting | bytes 2621440
  502.4 21.6 %copy.241 = f32[2,5,8,4096]{3,2,1,0:T(8,128)S(1)} copy(f32[2,5,8,4096]{2,0,1,3:T(2,128)} %bitcast.287) | data formatting | bytes 2621440 | tf_op jit(solution)/shard_map/all_to_all | solution.py:141
  525.5 2.7 copy_subtract_fusion
  528.9 7.8 %all-gather.1 = f32[8,1,128]{2,1,0:T(1,128)S(1)} all-gather(f32[2,1,128]{2,1,0:T(1,128)S(1)} %copy.246), channel_id=3, replica_groups=mesh['mode'=32,'wall'=2,'ckpt'=2] {'wall','ckpt'}, dimensions={0}, use_global_device_ids=true | all-gather | bytes 5120 | tf_op jit(solution)/shard_map/all_gather | solution.py:30
  (170 shorter events, 95.8 us)
Async XLA Ops:
  10.0 8.3 %copy-start.18 = (s32[128]{0:T(128)S(1)}, s32[128]{0:T(128)}, u32[]{:S(2)}) copy-start(s32[128]{0:T(128)} %param.9) | copy-start | bytes 1540
  10.0 52.0 %all-to-all-start.1 = ((f32[2,5,256,128]{3,1,0,2:T(8,128)}), f32[2,5,256,128]{3,1,0,2:T(8,128)S(1)}, u32[]{:S(2)}, u32[]{:S(2)}) async-start(f32[2,5,256,128]{3,1,0,2:T(8,128)} %copy.215), calls=%async_computation.1 | async-start | bytes 4194304 | tf_op jit(solution)/shard_map/all_to_all | solution.py:154
  17.6 42.1 %all-gather.5.cloned.1.call-start = ((), (), s32[]{:S(2)}) async-start(), calls=%async_computation.5 | async-start | bytes 1572864 | tf_op jit(solution)/shard_map/all_gather | solution.py:147
  62.0 32.9 %all-to-all-start = ((f32[2,2,256,128]{3,1,0,2:T(2,128)}), f32[2,2,256,128]{3,1,0,2:T(2,128)}, u32[]{:S(2)}, u32[]{:S(2)}) async-start(f32[2,2,256,128]{3,1,0,2:T(2,128)} %copy.211), calls=%async_computation | async-start | bytes 1048576 | tf_op jit(solution)/shard_map/all_to_all | solution.py:155
  79.1 1.3 copy-start.7
  80.5 4.0 copy-start.6
  105.8 1.0 copy-start.17
  122.8 1.3 copy-start.13
  186.0 7.6 %copy-start.4 = (f32[2,5,256,128]{3,2,1,0:T(8,128)S(1)}, f32[2,5,256,128]{3,2,1,0:T(8,128)}, u32[]{:S(2)}) copy-start(f32[2,5,256,128]{3,2,1,0:T(8,128)} %param.7) | copy-start | bytes 3932164
  186.0 27.3 %all-to-all-start.2 = ((f32[32,1,10240]{2,1,0:T(1,128)}), f32[32,1,10240]{2,1,0:T(1,128)}, u32[]{:S(2)}, u32[]{:S(2)}) async-start(f32[32,1,10240]{2,1,0:T(1,128)} %reshape.142), calls=%async_computation.2 | async-start | bytes 2621440 | tf_op jit(solution)/shard_map/all_to_all | solution.py:141
  193.6 8.2 %collective-permute-start = (f32[2,5,1,128]{3,0,2,1:T(2,128)S(1)}, f32[2,5,1,128]{3,0,2,1:T(2,128)S(1)}, u32[]{:S(2)}, u32[]{:S(2)}) collective-permute-start(f32[2,5,1,128]{3,0,2,1:T(2,128)S(1)} %copy.260), channel_id=1, source_target_pairs={{1,0},{2,1},{3,2},{5,4},{6,5},{7,6},{9,8},{10,9},{11,10},{13,12},{... | collective-permute-start | bytes 15368 | tf_op jit(solution)/shard_map/ppermute | solution.py:23
  194.9 7.7 %collective-permute-start.1 = (f32[2,5,1,128]{3,0,2,1:T(2,128)S(1)}, f32[2,5,1,128]{3,0,2,1:T(2,128)S(1)}, u32[]{:S(2)}, u32[]{:S(2)}) collective-permute-start(f32[2,5,1,128]{3,0,2,1:T(2,128)S(1)} %copy.261), channel_id=1, source_target_pairs={{0,1},{1,2},{2,3},{4,5},{5,6},{6,7},{8,9},{9,10},{10,11},{12,13},{... | collective-permute-start | bytes 15368 | tf_op jit(solution)/shard_map/ppermute | solution.py:20
  287.1 12.1 %copy-start.15 = (f32[2,1,256,128]{2,3,0,1:T(8,128)}, f32[2,1,256,128]{2,3,0,1:T(8,128)S(1)}, u32[]{:S(2)}) copy-start(f32[2,1,256,128]{2,3,0,1:T(8,128)S(1)} %slice.157) | copy-start | bytes 786436
  299.2 0.7 copy-start.16
  302.0 23.7 %all-to-all-start.3 = ((f32[2,5,256,128]{3,0,1,2:T(2,128)}), f32[2,5,256,128]{3,0,1,2:T(2,128)S(1)}, u32[]{:S(2)}, u32[]{:S(2)}) async-start(f32[2,5,256,128]{3,0,1,2:T(2,128)} %copy.232), calls=%async_computation.3 | async-start | bytes 2621440 | tf_op jit(solution)/shard_map/all_to_all | solution.py:164
  331.5 2.4 copy-start.9
  343.0 2.9 copy-start.3
  343.0 4.5 copy-start.5
  350.7 2.6 copy-start.14
  352.4 0.8 copy-start.2
  353.2 1.1 copy-start.8
  353.2 1.3 copy-start.10
  353.3 1.5 copy-start.11
  356.8 2.7 copy-start
  365.0 2.4 copy-start.1
  365.0 2.4 copy-start.12
  433.8 23.7 %all-to-all-start.4 = ((f32[32,1,10240]{2,1,0:T(1,128)}), f32[32,1,10240]{2,1,0:T(1,128)S(1)}, u32[]{:S(2)}, u32[]{:S(2)}) async-start(f32[32,1,10240]{2,1,0:T(1,128)} %reshape.144), calls=%async_computation.4 | async-start | bytes 2621440 | tf_op jit(solution)/shard_map/all_to_all | solution.py:141
  440.3 8.7 %collective-permute-start.2 = (f32[2,5,1,128]{3,0,2,1:T(2,128)S(1)}, f32[2,5,1,128]{3,0,2,1:T(2,128)S(1)}, u32[]{:S(2)}, u32[]{:S(2)}) collective-permute-start(f32[2,5,1,128]{3,0,2,1:T(2,128)S(1)} %copy.228), channel_id=1, source_target_pairs={{1,0},{2,1},{3,2},{5,4},{6,5},{7,6},{9,8},{10,9},{11,10},{13,12},{... | collective-permute-start | bytes 15368 | tf_op jit(solution)/shard_map/ppermute | solution.py:23
  442.9 7.4 %collective-permute-start.3 = (f32[2,5,1,128]{3,0,2,1:T(2,128)S(1)}, f32[2,5,1,128]{3,0,2,1:T(2,128)S(1)}, u32[]{:S(2)}, u32[]{:S(2)}) collective-permute-start(f32[2,5,1,128]{3,0,2,1:T(2,128)S(1)} %copy.230), channel_id=1, source_target_pairs={{0,1},{1,2},{2,3},{4,5},{5,6},{6,7},{8,9},{9,10},{10,11},{12,13},{... | collective-permute-start | bytes 15368 | tf_op jit(solution)/shard_map/ppermute | solution.py:20
Sparse Core Ops, SparseCore 0:
  20.1 27.8 all-gather.4
where the time goes:
time: 551 us; the launch traced here: 546 us
  local copies, waits for them, and re-layouts  296 us (54%)
  matrix products  87.6 us (16%)
  blocking collectives  59.1 us (11%)
  starting transfers between devices  44 us (8%)
  waiting for transfers between devices  27.5 us (5%)
  other arithmetic  16.9 us (3%)
  between operations  14.4 us (3%)
    unnamed x49, local copies, waits for them, and re-layouts  153 us
    all_to_all x3, local copies, waits for them, and re-layouts, to_modes(): lax.all_to_all(values, 'mode', split_axis=3, concat_axis=2, tiled=True)  43.7 us
    all_gather x1, blocking collectives, on_device(): full_map = lax.all_gather(mode_map, 'mode', axis=0, tiled=True)  40 us
    div x2, local copies, waits for them, and re-layouts, coupling_term(): return jnp.stack([real_part, imag_part]) / (NF * NK)  35.7 us
    all_gather x2, blocking collectives, entering(): pieces = lax.all_gather(value, axis)  19.1 us
    dot_general x5, matrix products, span_dft(): jnp.einsum('...k,kz->...z', imag_part, sine_part, precision=HIGHEST)  15.8 us
    all_to_all x2, waiting for transfers between devices, to_modes(): lax.all_to_all(values, 'mode', split_axis=3, concat_axis=2, tiled=True)  15.6 us
    dot_general x5, matrix products, span_dft(): real_cos = jnp.einsum('...k,kz->...z', real_part, cosine, precision=HIGHEST)  13.8 us
  transfers between devices with their start and end apart: 10, of which 5 were waited for; matrix products, arithmetic and copies ran while one was open for 9% of the time, Pallas kernels for 0%

commit v1 on v0

--- a/solution.py
+++ b/solution.py
@@ -10,6 +10,14 @@
 KAPPA = 0.2
 COUPLING = 0.5
 HIGHEST = lax.Precision.HIGHEST
+
+
+def clear_the_shapes(vals, ax_name):
+    reached = lax.psum(1, ax_name)
+    y = jnp.split(vals, reached, 3)
+    r_now = jnp.stack(y, axis=0)
+    r1 = lax.all_to_all(r_now, ax_name, 0, 0)
+    return jnp.concatenate(r1, 2)
 
 
 def with_halo(block, sides, width):
@@ -138,7 +146,7 @@
 
 
 def to_modes(values):
-    return lax.all_to_all(values, "mode", split_axis=3, concat_axis=2, tiled=True)
+    return clear_the_shapes(values, "mode")
 
 
 def on_device(adjoint, forward, mode_map):

time: 551 us -> 353 us (0.64)
  local copies, waits for them, and re-layouts: 296 us -> 109 us
  other arithmetic: 16.9 us -> 8.31 us
    unnamed x49 -> x105, local copies, waits for them, and re-layouts: 153 us -> 45.3 us
    all_to_all x3 -> x0, local copies, waits for them, and re-layouts: 43.7 us -> none  [to_modes(): lax.all_to_all(values, 'mode', split_axis=3, concat_axis=2, tiled=True)]
    div x2 -> x0, local copies, waits for them, and re-layouts: 35.7 us -> none  [coupling_term(): return jnp.stack([real_part, imag_part]) / (NF * NK)]
    all_to_all x2 -> x0, other arithmetic: 8.78 us -> none  [to_modes(): lax.all_to_all(values, 'mode', split_axis=3, concat_axis=2, tiled=True)]
  transfers between devices with their start and end apart: 10 -> 10, of which waited for: 5 -> 4; matrix products, arithmetic and copies ran while one was open for 9% -> 14% of each run, Pallas kernels for 0% -> 0%
where the time goes in v1:
time: 353 us; the launch traced here: 348 us
  local copies, waits for them, and re-layouts  109 us (31%)
  matrix products  86.2 us (24%)
  blocking collectives  59.1 us (17%)
  starting transfers between devices  44.5 us (13%)
  waiting for transfers between devices  26.7 us (8%)
  between operations  14.7 us (4%)
  other arithmetic  8.31 us (2%)
    unnamed x105, local copies, waits for them, and re-layouts  45.3 us
    all_gather x1, blocking collectives, on_device(): full_map = lax.all_gather(mode_map, 'mode', axis=0, tiled=True)  40 us
    all_gather x2, blocking collectives, entering(): pieces = lax.all_gather(value, axis)  19.1 us
    dot_general x5, matrix products, span_dft(): jnp.einsum('...k,kz->...z', imag_part, sine_part, precision=HIGHEST)  15.9 us
    all_to_all x2, waiting for transfers between devices, clear_the_shapes(): r1 = lax.all_to_all(r_now, ax_name, 0, 0)  15.4 us
    dot_general x5, matrix products, span_dft(): real_cos = jnp.einsum('...k,kz->...z', real_part, cosine, precision=HIGHEST)  13.8 us
    mul x10, local copies, waits for them, and re-layouts, coupling_term(): prod_real = w_real * a_real + w_imag * a_imag  13.2 us
    ppermute x2, starting transfers between devices, with_halo(): lax.ppermute(lax.slice_in_dim(block, block.shape[dim] - width, None, axis...  12.5 us
  transfers between devices with their start and end apart: 10, of which 4 were waited for; matrix products, arithmetic and copies ran while one was open for 14% of the time, Pallas kernels for 0%

profile of v1, /device:TPU:0, one launch (start us, length us, event | category | flops | bytes accessed | tf_op | source)
XLA Modules:
  0.0 348.2 jit_solution(16399125016380730434)
XLA Ops:
  6.5 3.5 copy.177
  10.0 7.6 %all-to-all-start.1 = ((f32[2,5,256,128]{3,1,0,2:T(8,128)}), f32[2,5,256,128]{3,1,0,2:T(8,128)S(1)}, u32[]{:S(2)}, u32[]{:S(2)}) async-start(f32[2,5,256,128]{3,1,0,2:T(8,128)} %copy.177), calls=%async_computation.1 | async-start | bytes 4194304 | tf_op jit(solution)/shard_map/all_to_all | solution.py:162
  18.3 40.0 %all-gather.2 = s32[32,1,128]{2,1,0:T(1,128)S(1)} all-gather(s32[1,1,128]{2,1,0:T(1,128)S(1)} %bitcast.535), channel_id=1, replica_groups=mesh['mode'=32,'wall'=2,'ckpt'=2] {'mode'}, dimensions={0}, use_global_device_ids=true | all-gather | bytes 16896 | tf_op jit(solution)/shard_map/all_gather | solution.py:158
  62.0 6.0 %all-to-all-start = ((f32[2,2,256,128]{3,1,0,2:T(2,128)}), f32[2,2,256,128]{3,1,0,2:T(2,128)}, u32[]{:S(2)}, u32[]{:S(2)}) async-start(f32[2,2,256,128]{3,1,0,2:T(2,128)} %copy.173), calls=%async_computation | async-start | bytes 1048576 | tf_op jit(solution)/shard_map/all_to_all | solution.py:163
  69.2 5.1 %fusion.66 = f32[64,5,8,64]{3,0,2,1:T(8,128)} fusion(f32[5,8,64,64]{3,2,1,0:T(8,128)S(1)} %reshape_squeeze.20), kind=kOutput, calls=%fused_computation.266 | convolution fusion | flops 125886464 | bytes 1310720 | tf_op jit(solution)/shard_map/...k,kz->...z/dot_general | solution.py:73
  74.3 5.1 %fusion.78 = f32[64,5,8,64]{3,0,2,1:T(8,128)} fusion(f32[5,8,64,64]{3,2,1,0:T(8,128)S(1)} %reshape_squeeze.20), kind=kOutput, calls=%fused_computation.278 | convolution fusion | flops 125886464 | bytes 1310720 | tf_op jit(solution)/shard_map/...k,kz->...z/dot_general | solution.py:74
  80.7 4.0 %convolution_subtract_fusion.7 = f32[64,5,8,64]{3,0,2,1:T(8,128)S(1)} fusion(f32[64,5,8,64]{3,0,2,1:T(8,128)S(1)} %copy-done.6, f32[5,8,64,64]{3,2,1,0:T(8,128)S(1)} %reshape_squeeze.21), kind=kOutput, calls=%fused_computation.17 | convolution fusion | flops 126050304 | bytes 1966080 | tf_op jit(solution)/shard_map/...k,kz->...z/dot_general | solution.py:76
  84.7 4.0 %convolution_add_fusion.7 = f32[64,5,8,64]{3,0,2,1:T(8,128)S(1)} fusion(f32[64,5,8,64]{3,0,2,1:T(8,128)S(1)} %copy-done.5, f32[5,8,64,64]{3,2,1,0:T(8,128)S(1)} %reshape_squeeze.21), kind=kOutput, calls=%fused_computation.16 | convolution fusion | flops 126050304 | bytes 1966080 | tf_op jit(solution)/shard_map/...k,kz->...z/dot_general | solution.py:75
  88.8 1.8 fusion.146
  92.3 2.5 convolution_add_fusion.3
  98.5 1.7 fusion.26
  112.9 3.2 multiply_subtract_fusion.1
  116.2 2.2 fusion.101
  120.4 2.4 fusion.21
  127.3 3.7 %convolution_subtract_fusion.6 = f32[5,8,64,64]{3,2,1,0:T(8,128)} fusion(f32[5,8,64,64]{3,2,1,0:T(8,128)} %fusion.21, f32[64,5,8,64]{3,2,1,0:T(8,128)S(1)} %reshape.115), kind=kOutput, calls=%fused_computation.15 | convolution fusion | flops 126054400 | bytes 1966080 | tf_op jit(solution)/shard_map/...k,kz->...z/dot_general | solution.py:76
  132.7 2.4 convolution_add_fusion.6
  156.9 7.5 %all-to-all-start.2 = ((f32[32,2,5,8,128]{4,3,2,1,0:T(8,128)}), f32[32,2,5,8,128]{4,3,2,1,0:T(8,128)}, u32[]{:S(2)}, u32[]{:S(2)}) async-start(f32[32,2,5,8,128]{4,3,2,1,0:T(8,128)} %constant_dynamic-update-slice_fusion), calls=%async_computation.2 | async-start | bytes 2621440 | tf_op jit(solution)/shard_map/all_to_all | solution.py:19
  165.8 6.4 %collective-permute-start.1 = (f32[2,5,1,128]{3,0,2,1:T(2,128)S(1)}, f32[2,5,1,128]{3,0,2,1:T(2,128)S(1)}, u32[]{:S(2)}, u32[]{:S(2)}) collective-permute-start(f32[2,5,1,128]{3,0,2,1:T(2,128)S(1)} %copy.219), channel_id=1, source_target_pairs={{0,1},{1,2},{2,3},{4,5},{5,6},{6,7},{8,9},{9,10},{10,11},{12,13},{... | collective-permute-start | bytes 15368 | tf_op jit(solution)/shard_map/ppermute | solution.py:28
  174.9 9.3 %all-to-all-done.2 = f32[32,2,5,8,128]{4,3,2,1,0:T(8,128)} async-done(((f32[32,2,5,8,128]{4,3,2,1,0:T(8,128)}), f32[32,2,5,8,128]{4,3,2,1,0:T(8,128)}, u32[]{:S(2)}, u32[]{:S(2)}) %all-to-all-start.2) | async-done | bytes 1310752 | tf_op jit(solution)/shard_map/all_to_all | solution.py:19
  187.1 2.6 fusion.9
  190.4 11.3 %all-gather = f32[8,1,128]{2,1,0:T(1,128)S(1)} all-gather(f32[2,1,128]{2,1,0:T(1,128)S(1)} %copy.187), channel_id=2, replica_groups=mesh['mode'=32,'wall'=2,'ckpt'=2] {'wall','ckpt'}, dimensions={0}, use_global_device_ids=true | all-gather | bytes 5120 | tf_op jit(solution)/shard_map/all_gather | solution.py:38
  202.8 2.1 copy.192
  204.9 4.1 %all-to-all-start.3 = ((f32[2,5,256,128]{3,0,1,2:T(2,128)}), f32[2,5,256,128]{3,0,1,2:T(2,128)S(1)}, u32[]{:S(2)}, u32[]{:S(2)}) async-start(f32[2,5,256,128]{3,0,1,2:T(2,128)} %copy.192), calls=%async_computation.3 | async-start | bytes 2621440 | tf_op jit(solution)/shard_map/all_to_all | solution.py:172
  209.0 2.1 mul.482
  211.1 2.5 mul.483
  213.6 2.1 mul.486
  215.7 2.5 mul.487
  218.2 10.4 %all-to-all-done.3 = f32[2,5,256,128]{3,0,1,2:T(2,128)S(1)} async-done(((f32[2,5,256,128]{3,0,1,2:T(2,128)}), f32[2,5,256,128]{3,0,1,2:T(2,128)S(1)}, u32[]{:S(2)}, u32[]{:S(2)}) %all-to-all-start.3) | async-done | bytes 1310752 | tf_op jit(solution)/shard_map/all_to_all | solution.py:172
  231.9 2.4 fusion.81
  234.4 2.4 fusion.71
  239.0 2.6 fusion
  241.6 1.8 copy.196
  243.5 2.5 reshape.116
  246.0 2.9 fusion.143
  251.8 1.8 copy.197
  257.8 1.8 fusion.100
  260.5 1.8 convolution_subtract_fusion
  263.6 2.5 fusion.15
  266.1 2.4 fusion.13
  271.6 3.8 %convolution_subtract_fusion.4 = f32[5,8,64,64]{3,2,1,0:T(8,128)} fusion(f32[5,8,64,64]{3,2,1,0:T(8,128)} %fusion.15, f32[64,5,8,64]{3,2,1,0:T(8,128)S(1)} %reshape.119), kind=kOutput, calls=%fused_computation.11 | convolution fusion | flops 126054400 | bytes 1966080 | tf_op jit(solution)/shard_map/...k,kz->...z/dot_general | solution.py:76
  275.4 2.6 stack_reshape.14
  277.9 3.7 %convolution_add_fusion.4 = f32[5,8,64,64]{3,2,1,0:T(8,128)} fusion(f32[5,8,64,64]{3,2,1,0:T(8,128)} %fusion.13, f32[64,5,8,64]{3,2,1,0:T(8,128)S(1)} %reshape.119), kind=kOutput, calls=%fused_computation.10 | convolution fusion | flops 126050304 | bytes 1966080 | tf_op jit(solution)/shard_map/...k,kz->...z/dot_general | solution.py:75
  281.7 1.8 stack_reshape.15
  303.5 4.2 %all-to-all-start.4 = ((f32[32,2,5,8,128]{4,3,2,1,0:T(8,128)}), f32[32,2,5,8,128]{4,3,2,1,0:T(8,128)S(1)}, u32[]{:S(2)}, u32[]{:S(2)}) async-start(f32[32,2,5,8,128]{4,3,2,1,0:T(8,128)} %constant_dynamic-update-slice_fusion.32), calls=%async_computation.4 | async-start | bytes 2621440 | tf_op jit(solution)/shard_map/all_to_all | solution.py:19
  313.0 6.1 %collective-permute-start.3 = (f32[2,5,1,128]{3,0,2,1:T(2,128)S(1)}, f32[2,5,1,128]{3,0,2,1:T(2,128)S(1)}, u32[]{:S(2)}, u32[]{:S(2)}) collective-permute-start(f32[2,5,1,128]{3,0,2,1:T(2,128)S(1)} %copy.190), channel_id=1, source_target_pairs={{0,1},{1,2},{2,3},{4,5},{5,6},{6,7},{8,9},{9,10},{10,11},{12,13},{... | collective-permute-start | bytes 15368 | tf_op jit(solution)/shard_map/ppermute | solution.py:28
  321.5 6.1 %all-to-all-done.4 = f32[32,2,5,8,128]{4,3,2,1,0:T(8,128)S(1)} async-done(((f32[32,2,5,8,128]{4,3,2,1,0:T(8,128)}), f32[32,2,5,8,128]{4,3,2,1,0:T(8,128)S(1)}, u32[]{:S(2)}, u32[]{:S(2)}) %all-to-all-start.4) | async-done | bytes 1310752 | tf_op jit(solution)/shard_map/all_to_all | solution.py:19
  328.1 2.7 copy_subtract_fusion
  331.4 7.8 %all-gather.1 = f32[8,1,128]{2,1,0:T(1,128)S(1)} all-gather(f32[2,1,128]{2,1,0:T(1,128)S(1)} %copy.204), channel_id=3, replica_groups=mesh['mode'=32,'wall'=2,'ckpt'=2] {'wall','ckpt'}, dimensions={0}, use_global_device_ids=true | all-gather | bytes 5120 | tf_op jit(solution)/shard_map/all_gather | solution.py:38
  (219 shorter events, 111.9 us)
Async XLA Ops:
  10.0 8.3 %copy-start.18 = (s32[128]{0:T(128)S(1)}, s32[128]{0:T(128)}, u32[]{:S(2)}) copy-start(s32[128]{0:T(128)} %param.9) | copy-start | bytes 1540
  10.0 52.0 %all-to-all-start.1 = ((f32[2,5,256,128]{3,1,0,2:T(8,128)}), f32[2,5,256,128]{3,1,0,2:T(8,128)S(1)}, u32[]{:S(2)}, u32[]{:S(2)}) async-start(f32[2,5,256,128]{3,1,0,2:T(8,128)} %copy.177), calls=%async_computation.1 | async-start | bytes 4194304 | tf_op jit(solution)/shard_map/all_to_all | solution.py:162
  17.6 42.1 %all-gather.5.cloned.1.call-start = ((), (), s32[]{:S(2)}) async-start(), calls=%async_computation.5 | async-start | bytes 1572864 | tf_op jit(solution)/shard_map/all_gather | solution.py:155
  62.0 32.7 %all-to-all-start = ((f32[2,2,256,128]{3,1,0,2:T(2,128)}), f32[2,2,256,128]{3,1,0,2:T(2,128)}, u32[]{:S(2)}, u32[]{:S(2)}) async-start(f32[2,2,256,128]{3,1,0,2:T(2,128)} %copy.173), calls=%async_computation | async-start | bytes 1048576 | tf_op jit(solution)/shard_map/all_to_all | solution.py:163
  79.4 1.3 copy-start.6
  80.7 4.0 %copy-start.5 = (f32[64,5,8,64]{3,0,2,1:T(8,128)S(1)}, f32[64,5,8,64]{3,0,2,1:T(8,128)}, u32[]{:S(2)}) copy-start(f32[64,5,8,64]{3,0,2,1:T(8,128)} %fusion.78) | copy-start | bytes 1966084
  105.7 1.0 copy-start.17
  122.8 1.3 copy-start.12
  156.9 7.6 %copy-start.3 = (f32[2,5,256,128]{3,2,1,0:T(8,128)S(1)}, f32[2,5,256,128]{3,2,1,0:T(8,128)}, u32[]{:S(2)}) copy-start(f32[2,5,256,128]{3,2,1,0:T(8,128)} %param.7) | copy-start | bytes 3932164
  156.9 27.3 %all-to-all-start.2 = ((f32[32,2,5,8,128]{4,3,2,1,0:T(8,128)}), f32[32,2,5,8,128]{4,3,2,1,0:T(8,128)}, u32[]{:S(2)}, u32[]{:S(2)}) async-start(f32[32,2,5,8,128]{4,3,2,1,0:T(8,128)} %constant_dynamic-update-slice_fusion), calls=%async_computation.2 | async-start | bytes 2621440 | tf_op jit(solution)/shard_map/all_to_all | solution.py:19
  164.5 8.2 %collective-permute-start = (f32[2,5,1,128]{3,0,2,1:T(2,128)S(1)}, f32[2,5,1,128]{3,0,2,1:T(2,128)S(1)}, u32[]{:S(2)}, u32[]{:S(2)}) collective-permute-start(f32[2,5,1,128]{3,0,2,1:T(2,128)S(1)} %copy.218), channel_id=1, source_target_pairs={{1,0},{2,1},{3,2},{5,4},{6,5},{7,6},{9,8},{10,9},{11,10},{13,12},{... | collective-permute-start | bytes 15368 | tf_op jit(solution)/shard_map/ppermute | solution.py:31
  165.8 8.0 %collective-permute-start.1 = (f32[2,5,1,128]{3,0,2,1:T(2,128)S(1)}, f32[2,5,1,128]{3,0,2,1:T(2,128)S(1)}, u32[]{:S(2)}, u32[]{:S(2)}) collective-permute-start(f32[2,5,1,128]{3,0,2,1:T(2,128)S(1)} %copy.219), channel_id=1, source_target_pairs={{0,1},{1,2},{2,3},{4,5},{5,6},{6,7},{8,9},{9,10},{10,11},{12,13},{... | collective-permute-start | bytes 15368 | tf_op jit(solution)/shard_map/ppermute | solution.py:28
  189.9 12.1 %copy-start.15 = (f32[2,1,256,128]{2,3,0,1:T(8,128)}, f32[2,1,256,128]{2,3,0,1:T(8,128)S(1)}, u32[]{:S(2)}) copy-start(f32[2,1,256,128]{2,3,0,1:T(8,128)S(1)} %slice.157) | copy-start | bytes 786436
  202.0 0.7 copy-start.16
  204.9 23.7 %all-to-all-start.3 = ((f32[2,5,256,128]{3,0,1,2:T(2,128)}), f32[2,5,256,128]{3,0,1,2:T(2,128)S(1)}, u32[]{:S(2)}, u32[]{:S(2)}) async-start(f32[2,5,256,128]{3,0,1,2:T(2,128)} %copy.192), calls=%async_computation.3 | async-start | bytes 2621440 | tf_op jit(solution)/shard_map/all_to_all | solution.py:172
  234.4 2.4 copy-start.8
  246.0 2.9 copy-start.2
  246.0 4.6 %copy-start.4 = (f32[5,8,64,64]{3,2,1,0:T(8,128)S(1)}, f32[5,8,64,64]{3,2,1,0:T(8,128)}, u32[]{:S(2)}) copy-start(f32[5,8,64,64]{3,2,1,0:T(8,128)} %fusion.81) | copy-start | bytes 1966084
  253.6 1.7 copy-start.13
  255.4 1.1 copy-start.7
  255.4 1.3 copy-start.9
  255.4 1.5 copy-start.10
  257.8 2.7 copy-start
  266.1 2.4 copy-start.1
  266.1 2.4 copy-start.11
  281.7 1.8 copy-start.14
  303.5 24.0 %all-to-all-start.4 = ((f32[32,2,5,8,128]{4,3,2,1,0:T(8,128)}), f32[32,2,5,8,128]{4,3,2,1,0:T(8,128)S(1)}, u32[]{:S(2)}, u32[]{:S(2)}) async-start(f32[32,2,5,8,128]{4,3,2,1,0:T(8,128)} %constant_dynamic-update-slice_fusion.32), calls=%async_computation.4 | async-start | bytes 2621440 | tf_op jit(solution)/shard_map/all_to_all | solution.py:19
  310.4 8.7 %collective-permute-start.2 = (f32[2,5,1,128]{3,0,2,1:T(2,128)S(1)}, f32[2,5,1,128]{3,0,2,1:T(2,128)S(1)}, u32[]{:S(2)}, u32[]{:S(2)}) collective-permute-start(f32[2,5,1,128]{3,0,2,1:T(2,128)S(1)} %copy.188), channel_id=1, source_target_pairs={{1,0},{2,1},{3,2},{5,4},{6,5},{7,6},{9,8},{10,9},{11,10},{13,12},{... | collective-permute-start | bytes 15368 | tf_op jit(solution)/shard_map/ppermute | solution.py:31
  313.0 7.4 %collective-permute-start.3 = (f32[2,5,1,128]{3,0,2,1:T(2,128)S(1)}, f32[2,5,1,128]{3,0,2,1:T(2,128)S(1)}, u32[]{:S(2)}, u32[]{:S(2)}) collective-permute-start(f32[2,5,1,128]{3,0,2,1:T(2,128)S(1)} %copy.190), channel_id=1, source_target_pairs={{0,1},{1,2},{2,3},{4,5},{5,6},{6,7},{8,9},{9,10},{10,11},{12,13},{... | collective-permute-start | bytes 15368 | tf_op jit(solution)/shard_map/ppermute | solution.py:28
Sparse Core Ops, SparseCore 0:
  20.0 27.8 all-gather.4
